TPU v7x, 32 devices: a whole 2x2x4 slice. The times are simulated.
32 devices in a mesh: row: 8 (over z, y), col: 4 (over x, core).
Axes of the slice: x: 2, y: 2, z: 4, core: 2. Of those that a mesh axis runs over, the one named last changes fastest.
Arguments:
- rhs: float32 [32768, 256], P(('row', 'col')), may hold values from -6 to 6
- local_mat: bfloat16 [32768, 1024], P(('row', 'col')), may hold values from -1 to 5
- local_inv: bfloat16 [32768, 1024], P(('row', 'col')), may hold values from -1 to 1
- basis_t: bfloat16 [3072, 1024], P(('row', 'col')), may hold values from -0.1875 to 0.1875
- coarse_inv: bfloat16 [3072, 3072], P('col', 'row'), may hold values from -0.109375 to 0.109375
- couple: float32 [32, 4, 128], P(('row', 'col')), may hold values from 0.5 to 2
- margin_rows: int32 [32, 4, 128], P(('row', 'col')), may hold values from 0 to 1023, as said below
Outputs:
- solution: float32 [32768, 256], P(('row', 'col'))
- residual: float32 [32768, 256], P(('row', 'col'))
Inputs may be any that keep to these rules, and one draw needn't show every extreme that they name: `margin_rows`: within each subdomain the 512 listed rows are all different.
All inputs are finite; a program needn't handle non-finite values.
Results may differ from a plain program's by a relative error of at most 0.024.
Values may be sent and summed in bfloat16 or wider, within the bound.
No kernel may reach another device: no remote copies, remote signals or barrier semaphores. Data moves between devices by JAX's collectives and lax.ppermute only.
A program may use at most 64 MiB of HBM per device.

v0:
```python
import jax
import jax.numpy as jnp
from jax import lax
from jax.sharding import PartitionSpec as P

STEPS = 2


def padded(cells, sides, width):
    for axis, dim in sides:
        count = lax.axis_size(axis)
        ends = count - 1
        head = lax.slice_in_dim(cells, 0, width, axis=dim)
        tail = lax.slice_in_dim(cells, cells.shape[dim] - width, cells.shape[dim], axis=dim)
        cells = jnp.concatenate(
            [
                lax.ppermute(tail, axis, [(i, (i + 1) % count) for i in range(ends)]),
                cells,
                lax.ppermute(head, axis, [((i + 1) % count, i) for i in range(ends)]),
            ],
            axis=dim,
        )
    return cells


def per_device(rhs, local_mat, local_inv, basis_t, coarse_inv, couple, margin_rows):
    face_index = margin_rows[0]
    flat_rows = face_index.reshape(-1)
    weights = couple[0]
    columns = rhs.shape[1]

    def neighbour_faces(vector_b):
        face_vals = vector_b[face_index]
        north_south = padded(face_vals[0:2], (("row", 0),), 1)
        west_east = padded(face_vals[2:4], (("col", 0),), 1)
        received = jnp.stack([north_south[0], north_south[3], west_east[0], west_east[3]])
        return received

    def apply_operator(vector):
        vector_b = vector.astype(jnp.bfloat16)
        received = neighbour_faces(vector_b)
        coupling_terms = (weights[:, :, None] * received.astype(jnp.float32)).reshape(-1, columns)
        coupled = jnp.zeros(vector.shape, jnp.float32).at[flat_rows].add(coupling_terms)
        return jnp.dot(local_mat, vector_b, preferred_element_type=jnp.float32) - coupled

    solution = jnp.zeros(rhs.shape, jnp.float32)
    residual = rhs
    for sweep in range(STEPS):
        if sweep > 0:
            residual = rhs - apply_operator(solution)
        rounded = residual.astype(jnp.bfloat16)
        restricted = jnp.dot(basis_t, rounded, preferred_element_type=jnp.float32).astype(
            jnp.bfloat16
        )
        block_rows = restricted.shape[0]
        partial_sum = jnp.dot(
            coarse_inv,
            lax.all_gather(restricted, "col", axis=0, tiled=True),
            preferred_element_type=jnp.float32,
        )
        summed = lax.psum(partial_sum, "row")
        coarse_part = lax.dynamic_slice_in_dim(
            summed, lax.axis_index("row") * block_rows, block_rows, 0
        )
        coarse_b = coarse_part.astype(jnp.bfloat16)
        solution = solution + lax.dot_general(
            basis_t, coarse_b, (((0,), (0,)), ((), ())), preferred_element_type=jnp.float32
        )
        residual = rhs - apply_operator(solution)
        solution = solution + jnp.dot(
            local_inv, residual.astype(jnp.bfloat16), preferred_element_type=jnp.float32
        )
    residual = rhs - apply_operator(solution)
    return (solution, residual)


def solution(mesh):
    placed = (
        P(("row", "col"), None),
        P(("row", "col"), None),
        P(("row", "col"), None),
        P(("row", "col"), None),
        P("col", "row"),
        P(("row", "col"), None, None),
        P(("row", "col"), None, None),
    )
    return jax.shard_map(
        per_device,
        mesh=mesh,
        in_specs=placed,
        out_specs=(P(("row", "col"), None), P(("row", "col"), None)),
        check_vma=False,
    )
```

profile of v0, /device:TPU:9, one launch (start us, length us, event | category | flops | bytes accessed | tf_op | source)
XLA Modules:
  0.0 242.6 jit_solution(8589869174017089495)
XLA Ops:
  3.1 6.1 %all_gather.6 = bf16[384,256]{1,0:T(8,128)(2,1)S(1)} all-gather(bf16[96,256]{1,0:T(8,128)(2,1)S(1)} %convolution_convert_fusion), channel_id=1, replica_groups=mesh['row'=8,'col'=4] {'col'}, dimensions={0}, use_global_device_ids=true | all-gather | bytes 245760 | tf_op jit(solution)/shard_map/all_gather | solution.py:58
  10.7 40.2 %all-reduce.2 = bf16[768,256]{0,1:T(8,128)(2,1)} all-reduce(f32[768,256]{0,1:T(8,128)S(1)} %convolution_bitcast_fusion.5), channel_id=1, replica_groups=mesh['row'=8,'col'=4] {'row'}, use_global_device_ids=true, to_apply=%region_0.0 | all-reduce | flops 196608 | bytes 1179648 | tf_op jit(solution)/shard_map/psum | solution.py:61
  53.4 2.0 gather_fusion
  56.0 1.9 collective-permute-start
  57.9 8.7 %collective-permute-start.2 = (bf16[1,128,256]{2,1,0:T(8,128)(2,1)}, bf16[1,128,256]{2,1,0:T(8,128)(2,1)}, u32[]{:S(2)}, u32[]{:S(2)}) collective-permute-start(bf16[1,128,256]{2,1,0:T(8,128)(2,1)} %get-tuple-element.21), channel_id=1, source_target_pairs={{0,1},{1,2},{2,3},{4,5},{5,6},{6,7},{8,9},{9,10},{10,11},{12,13},{... | collective-permute-start | bytes 196616 | tf_op jit(solution)/shard_map/ppermute | solution.py:17
  66.6 3.3 %collective-permute-start.1 = (bf16[1,128,256]{2,1,0:T(8,128)(2,1)S(1)}, bf16[1,128,256]{2,1,0:T(8,128)(2,1)}, u32[]{:S(2)}, u32[]{:S(2)}) collective-permute-start(bf16[1,128,256]{2,1,0:T(8,128)(2,1)S(1)} %get-tuple-element.22), channel_id=1, source_target_pairs={{4,0},{8,4},{12,8},{16,12},{20,16},{24,20},{28,24},{5,1},{9,5},{13... | collective-permute-start | bytes 196616 | tf_op jit(solution)/shard_map/ppermute | solution.py:19
  69.9 1.9 collective-permute-start.3
  73.5 2.1 collective-permute-done.3
  75.6 1.6 pad_maximum_fusion
  77.3 4.8 %scatter_custom_fusion = f32[1024,256]{1,0:T(8,128)} fusion(s32[512]{0:T(512)S(1)} %bitcast.127, bf16[512,256]{1,0:T(8,128)(2,1)} %bitcast.119, f32[]{:T(128)} %constant.4.clone.1, f32[512]{0:T(512)S(1)} %bitcast.122), kind=kCustom, calls=%fused_computation.40 | custom fusion | flops 393216 | bytes 1312772 | tf_op jit(solution)/shard_map/scatter-add | solution.py:43
  82.1 2.5 %copy.32 = f32[1024,256]{0,1:T(8,128)} copy(f32[1024,256]{1,0:T(8,128)} %scatter_custom_fusion) | data formatting | bytes 2097152 | tf_op jit(solution)/shard_map/scatter-add | solution.py:43
  84.6 4.8 %convolution_add_fusion.2 = f32[256,1024]{1,0:T(8,128)} fusion(f32[256,1024]{1,0:T(8,128)} %copy-done.2, bf16[1024,1024]{1,0:T(8,128)(2,1)} %param.9, f32[1024,256]{0,1:T(8,128)S(1)} %copy.33, f32[1024,256]{0,1:T(8,128)} %copy.32, bf16[1024,1024]{1,0:T(8,128)(2,1)S(1)} %copy-done), kind=kOutput, calls=%fused_computation.23 | convolution fusion | flops 1075052544 | bytes 8388608 | tf_op jit(solution)/shard_map/dot_general | solution.py:70
  89.4 2.1 convert_bitcast_fusion.1
  91.5 2.0 copy.34
  93.5 3.3 %gather_fusion.1 = bf16[512,256]{1,0:T(8,128)(2,1)} fusion(bf16[1024,256]{1,0:T(8,128)(2,1)} %copy.34, s32[1024]{0:T(1024)S(1)} %pad_clamp_fusion), kind=kCustom, calls=%fused_computation.1 | custom fusion | bytes 526336 | tf_op jit(solution)/shard_map/gather | solution.py:33
  97.8 1.9 collective-permute-start.4
  99.7 2.0 collective-permute-start.6
  101.8 4.2 %collective-permute-start.5 = (bf16[1,128,256]{2,1,0:T(8,128)(2,1)S(1)}, bf16[1,128,256]{2,1,0:T(8,128)(2,1)S(1)}, u32[]{:S(2)}, u32[]{:S(2)}) collective-permute-start(bf16[1,128,256]{2,1,0:T(8,128)(2,1)S(1)} %get-tuple-element.18), channel_id=1, source_target_pairs={{4,0},{8,4},{12,8},{16,12},{20,16},{24,20},{28,24},{5,1},{9,5},{13... | collective-permute-start | bytes 196616 | tf_op jit(solution)/shard_map/ppermute | solution.py:19
  106.0 2.6 %collective-permute-start.7 = (bf16[1,128,256]{2,1,0:T(8,128)(2,1)S(1)}, bf16[1,128,256]{2,1,0:T(8,128)(2,1)S(1)}, u32[]{:S(2)}, u32[]{:S(2)}) collective-permute-start(bf16[1,128,256]{2,1,0:T(8,128)(2,1)S(1)} %get-tuple-element.19), channel_id=1, source_target_pairs={{1,0},{2,1},{3,2},{5,4},{6,5},{7,6},{9,8},{10,9},{11,10},{13,12},{... | collective-permute-start | bytes 196616 | tf_op jit(solution)/shard_map/ppermute | solution.py:19
  108.6 3.0 %collective-permute-done.7 = bf16[1,128,256]{2,1,0:T(8,128)(2,1)S(1)} collective-permute-done((bf16[1,128,256]{2,1,0:T(8,128)(2,1)S(1)}, bf16[1,128,256]{2,1,0:T(8,128)(2,1)S(1)}, u32[]{:S(2)}, u32[]{:S(2)}) %collective-permute-start.7) | collective-permute-done | bytes 65568 | tf_op jit(solution)/shard_map/ppermute | solution.py:19
  112.3 4.8 %scatter_custom_fusion.1 = f32[1024,256]{1,0:T(8,128)} fusion(s32[512]{0:T(512)S(1)} %bitcast.128, bf16[512,256]{1,0:T(8,128)(2,1)} %bitcast.120, f32[]{:T(128)} %constant.4.clone.1, f32[512]{0:T(512)S(1)} %bitcast.123), kind=kCustom, calls=%fused_computation.38 | custom fusion | flops 393216 | bytes 1312772 | tf_op jit(solution)/shard_map/scatter-add | solution.py:43
  117.1 2.5 %copy.35 = f32[1024,256]{0,1:T(8,128)} copy(f32[1024,256]{1,0:T(8,128)} %scatter_custom_fusion.1) | data formatting | bytes 2097152 | tf_op jit(solution)/shard_map/scatter-add | solution.py:43
  119.7 2.5 %fusion.14 = bf16[96,256]{1,0:T(8,128)(2,1)S(1)} fusion(bf16[96,1024]{1,0:T(8,128)(2,1)S(1)} %copy-done.3, f32[1024,256]{0,1:T(8,128)S(1)} %copy.33, f32[1024,256]{0,1:T(8,128)} %copy.35, bf16[1024,1024]{1,0:T(8,128)(2,1)S(1)} %copy-done, f32[256,1024]{1,0:T(8,128)} %convolution_add_fusion.2), kind=kOutput, calls=%fused_computation.32 | convolution fusion | flops 588275712 | bytes 5488640 | tf_op jit(solution)/shard_map/dot_general | solution.py:52
  122.2 4.4 %all_gather.7 = bf16[384,256]{1,0:T(8,128)(2,1)S(1)} all-gather(bf16[96,256]{1,0:T(8,128)(2,1)S(1)} %fusion.14), channel_id=1, replica_groups=mesh['row'=8,'col'=4] {'col'}, dimensions={0}, use_global_device_ids=true | all-gather | bytes 245760 | tf_op jit(solution)/shard_map/all_gather | solution.py:58
  126.6 2.4 convolution_bitcast_fusion.4
  129.0 39.4 %all-reduce.3 = bf16[768,256]{0,1:T(8,128)(2,1)} all-reduce(f32[768,256]{0,1:T(8,128)} %convolution_bitcast_fusion.4), channel_id=1, replica_groups=mesh['row'=8,'col'=4] {'row'}, use_global_device_ids=true, to_apply=%region_3.0 | all-reduce | flops 196608 | bytes 1179648 | tf_op jit(solution)/shard_map/psum | solution.py:61
  168.4 1.6 convolution_add_fusion
  171.9 2.0 copy.37
  173.9 2.7 %gather_fusion.2 = bf16[512,256]{1,0:T(8,128)(2,1)S(1)} fusion(bf16[1024,256]{1,0:T(8,128)(2,1)} %copy.37, s32[1024]{0:T(1024)S(1)} %pad_clamp_fusion), kind=kCustom, calls=%fused_computation.2 | custom fusion | bytes 526336 | tf_op jit(solution)/shard_map/gather | solution.py:33
  176.6 1.9 collective-permute-start.8
  178.6 8.4 %collective-permute-start.10 = (bf16[1,128,256]{2,1,0:T(8,128)(2,1)S(1)}, bf16[1,128,256]{2,1,0:T(8,128)(2,1)S(1)}, u32[]{:S(2)}, u32[]{:S(2)}) collective-permute-start(bf16[1,128,256]{2,1,0:T(8,128)(2,1)S(1)} %get-tuple-element.13), channel_id=1, source_target_pairs={{0,1},{1,2},{2,3},{4,5},{5,6},{6,7},{8,9},{9,10},{10,11},{12,13},{... | collective-permute-start | bytes 196616 | tf_op jit(solution)/shard_map/ppermute | solution.py:17
  187.0 4.5 %collective-permute-start.9 = (bf16[1,128,256]{2,1,0:T(8,128)(2,1)S(1)}, bf16[1,128,256]{2,1,0:T(8,128)(2,1)S(1)}, u32[]{:S(2)}, u32[]{:S(2)}) collective-permute-start(bf16[1,128,256]{2,1,0:T(8,128)(2,1)S(1)} %get-tuple-element.14), channel_id=1, source_target_pairs={{4,0},{8,4},{12,8},{16,12},{20,16},{24,20},{28,24},{5,1},{9,5},{13... | collective-permute-start | bytes 196616 | tf_op jit(solution)/shard_map/ppermute | solution.py:19
  191.5 1.9 collective-permute-start.11
  193.5 3.6 %collective-permute-done.11 = bf16[1,128,256]{2,1,0:T(8,128)(2,1)S(1)} collective-permute-done((bf16[1,128,256]{2,1,0:T(8,128)(2,1)S(1)}, bf16[1,128,256]{2,1,0:T(8,128)(2,1)S(1)}, u32[]{:S(2)}, u32[]{:S(2)}) %collective-permute-start.11) | collective-permute-done | bytes 65568 | tf_op jit(solution)/shard_map/ppermute | solution.py:19
  197.2 4.4 %scatter_custom_fusion.2 = f32[1024,256]{1,0:T(8,128)} fusion(s32[512]{0:T(512)S(1)} %bitcast.129, bf16[512,256]{1,0:T(8,128)(2,1)S(1)} %bitcast.121, f32[]{:T(128)} %constant.4.clone.1, f32[512]{0:T(512)S(1)} %bitcast.124), kind=kCustom, calls=%fused_computation.36 | custom fusion | flops 393216 | bytes 1312772 | tf_op jit(solution)/shard_map/scatter-add | solution.py:43
  201.6 2.6 %copy.38 = f32[1024,256]{0,1:T(8,128)} copy(f32[1024,256]{1,0:T(8,128)} %scatter_custom_fusion.2) | data formatting | bytes 2097152 | tf_op jit(solution)/shard_map/scatter-add | solution.py:43
  204.2 5.0 %fusion.38 = (bf16[1024,256]{0,1:T(8,128)(2,1)}, f32[1024,256]{0,1:T(8,128)}) fusion(f32[256,1024]{1,0:T(8,128)} %copy-done.1, bf16[1024,1024]{1,0:T(8,128)(2,1)} %param.9, f32[1024,256]{0,1:T(8,128)S(1)} %copy.33, f32[1024,256]{0,1:T(8,128)} %copy.38, bf16[1024,1024]{1,0:T(8,128)(2,1)S(1)} %copy-done), kind=kOutput, calls=%fused_computation.85 | convolution fusion | flops 1075314688 | bytes 8912896 | tf_op jit(solution)/shard_map/dot_general | solution.py:70
  209.1 2.0 copy.40
  211.2 2.7 %gather_fusion.3 = bf16[512,256]{1,0:T(8,128)(2,1)S(1)} fusion(bf16[1024,256]{1,0:T(8,128)(2,1)} %copy.40, s32[1024]{0:T(1024)S(1)} %pad_clamp_fusion), kind=kCustom, calls=%fused_computation.3 | custom fusion | bytes 526336 | tf_op jit(solution)/shard_map/gather | solution.py:33
  214.5 1.9 collective-permute-start.12
  216.4 1.9 collective-permute-start.14
  218.3 4.5 %collective-permute-start.13 = (bf16[1,128,256]{2,1,0:T(8,128)(2,1)}, bf16[1,128,256]{2,1,0:T(8,128)(2,1)S(1)}, u32[]{:S(2)}, u32[]{:S(2)}) collective-permute-start(bf16[1,128,256]{2,1,0:T(8,128)(2,1)} %get-tuple-element.10), channel_id=1, source_target_pairs={{4,0},{8,4},{12,8},{16,12},{20,16},{24,20},{28,24},{5,1},{9,5},{13... | collective-permute-start | bytes 196616 | tf_op jit(solution)/shard_map/ppermute | solution.py:19
  222.8 2.5 %collective-permute-start.15 = (bf16[1,128,256]{2,1,0:T(8,128)(2,1)S(1)}, bf16[1,128,256]{2,1,0:T(8,128)(2,1)}, u32[]{:S(2)}, u32[]{:S(2)}) collective-permute-start(bf16[1,128,256]{2,1,0:T(8,128)(2,1)S(1)} %get-tuple-element.11), channel_id=1, source_target_pairs={{1,0},{2,1},{3,2},{5,4},{6,5},{7,6},{9,8},{10,9},{11,10},{13,12},{... | collective-permute-start | bytes 196616 | tf_op jit(solution)/shard_map/ppermute | solution.py:19
  225.3 2.5 %copy.43 = f32[1024,256]{1,0:T(8,128)} copy(f32[1024,256]{0,1:T(8,128)} %get-tuple-element.25) | data formatting | bytes 2097152
  230.0 4.4 %scatter_custom_fusion.3 = f32[1024,256]{1,0:T(8,128)} fusion(s32[512]{0:T(512)S(1)} %bitcast.130, bf16[512,256]{1,0:T(8,128)(2,1)S(1)} %bitcast.118, f32[]{:T(128)} %constant.4.clone.1, f32[512]{0:T(512)S(1)} %bitcast.125), kind=kCustom, calls=%fused_computation.34 | custom fusion | flops 393216 | bytes 1312772 | tf_op jit(solution)/shard_map/scatter-add | solution.py:43
  234.5 2.5 %copy.41 = f32[1024,256]{0,1:T(8,128)} copy(f32[1024,256]{1,0:T(8,128)} %scatter_custom_fusion.3) | data formatting | bytes 2097152 | tf_op jit(solution)/shard_map/scatter-add | solution.py:43
  237.0 3.1 %fusion.7 = f32[1024,256]{0,1:T(8,128)} fusion(f32[1024,256]{0,1:T(8,128)S(1)} %copy.33, f32[1024,256]{0,1:T(8,128)} %copy.41, bf16[1024,256]{0,1:T(8,128)(2,1)} %get-tuple-element.24, bf16[1024,1024]{1,0:T(8,128)(2,1)S(1)} %copy-done), kind=kOutput, calls=%fused_computation.20 | convolution fusion | flops 537395200 | bytes 5767168 | tf_op jit(solution)/shard_map/dot_general | solution.py:44
  240.1 2.5 %copy.44 = f32[1024,256]{1,0:T(8,128)} copy(f32[1024,256]{0,1:T(8,128)} %fusion.7) | data formatting | bytes 2097152
  (46 shorter events, 15.1 us)
Async XLA Ops:
  0.6 84.0 %copy-start = (bf16[1024,1024]{1,0:T(8,128)(2,1)S(1)}, bf16[1024,1024]{1,0:T(8,128)(2,1)}, u32[]{:S(2)}) copy-start(bf16[1024,1024]{1,0:T(8,128)(2,1)} %param.8) | copy-start | bytes 6291460
  1.5 49.4 %copy-start.3 = (bf16[96,1024]{1,0:T(8,128)(2,1)S(1)}, bf16[96,1024]{1,0:T(8,128)(2,1)}, u32[]{:S(2)}) copy-start(bf16[96,1024]{1,0:T(8,128)(2,1)} %param.10) | copy-start | bytes 589828
  52.1 1.0 copy-start.2
  53.1 18.7 %copy-start.7 = (s32[1,4,128]{2,1,0:T(4,128)S(1)}, s32[1,4,128]{2,1,0:T(4,128)}, u32[]{:S(2)}) copy-start(s32[1,4,128]{2,1,0:T(4,128)} %param.13) | copy-start | bytes 6148
  55.3 21.9 %copy-start.6 = (f32[1,4,128]{2,1,0:T(4,128)S(1)}, f32[1,4,128]{2,1,0:T(4,128)}, u32[]{:S(2)}) copy-start(f32[1,4,128]{2,1,0:T(4,128)} %param.12) | copy-start | bytes 6148
  56.0 17.5 %collective-permute-start = (bf16[1,128,256]{2,1,0:T(8,128)(2,1)}, bf16[1,128,256]{2,1,0:T(8,128)(2,1)S(1)}, u32[]{:S(2)}, u32[]{:S(2)}) collective-permute-start(bf16[1,128,256]{2,1,0:T(8,128)(2,1)} %get-tuple-element.20), channel_id=1, source_target_pairs={{0,4},{4,8},{8,12},{12,16},{16,20},{20,24},{24,28},{1,5},{5,9},{9,... | collective-permute-start | bytes 196616 | tf_op jit(solution)/shard_map/ppermute | solution.py:17
  57.9 15.6 %collective-permute-start.2 = (bf16[1,128,256]{2,1,0:T(8,128)(2,1)}, bf16[1,128,256]{2,1,0:T(8,128)(2,1)}, u32[]{:S(2)}, u32[]{:S(2)}) collective-permute-start(bf16[1,128,256]{2,1,0:T(8,128)(2,1)} %get-tuple-element.21), channel_id=1, source_target_pairs={{0,1},{1,2},{2,3},{4,5},{5,6},{6,7},{8,9},{9,10},{10,11},{12,13},{... | collective-permute-start | bytes 196616 | tf_op jit(solution)/shard_map/ppermute | solution.py:17
  66.6 6.9 %collective-permute-start.1 = (bf16[1,128,256]{2,1,0:T(8,128)(2,1)S(1)}, bf16[1,128,256]{2,1,0:T(8,128)(2,1)}, u32[]{:S(2)}, u32[]{:S(2)}) collective-permute-start(bf16[1,128,256]{2,1,0:T(8,128)(2,1)S(1)} %get-tuple-element.22), channel_id=1, source_target_pairs={{4,0},{8,4},{12,8},{16,12},{20,16},{24,20},{28,24},{5,1},{9,5},{13... | collective-permute-start | bytes 196616 | tf_op jit(solution)/shard_map/ppermute | solution.py:19
  69.9 5.7 %collective-permute-start.3 = (bf16[1,128,256]{2,1,0:T(8,128)(2,1)S(1)}, bf16[1,128,256]{2,1,0:T(8,128)(2,1)}, u32[]{:S(2)}, u32[]{:S(2)}) collective-permute-start(bf16[1,128,256]{2,1,0:T(8,128)(2,1)S(1)} %get-tuple-element.23), channel_id=1, source_target_pairs={{1,0},{2,1},{3,2},{5,4},{6,5},{7,6},{9,8},{10,9},{11,10},{13,12},{... | collective-permute-start | bytes 196616 | tf_op jit(solution)/shard_map/ppermute | solution.py:19
  97.8 10.8 %collective-permute-start.4 = (bf16[1,128,256]{2,1,0:T(8,128)(2,1)S(1)}, bf16[1,128,256]{2,1,0:T(8,128)(2,1)S(1)}, u32[]{:S(2)}, u32[]{:S(2)}) collective-permute-start(bf16[1,128,256]{2,1,0:T(8,128)(2,1)S(1)} %get-tuple-element.16), channel_id=1, source_target_pairs={{0,4},{4,8},{8,12},{12,16},{16,20},{20,24},{24,28},{1,5},{5,9},{9,... | collective-permute-start | bytes 196616 | tf_op jit(solution)/shard_map/ppermute | solution.py:17
  99.7 8.9 %collective-permute-start.6 = (bf16[1,128,256]{2,1,0:T(8,128)(2,1)S(1)}, bf16[1,128,256]{2,1,0:T(8,128)(2,1)S(1)}, u32[]{:S(2)}, u32[]{:S(2)}) collective-permute-start(bf16[1,128,256]{2,1,0:T(8,128)(2,1)S(1)} %get-tuple-element.17), channel_id=1, source_target_pairs={{0,1},{1,2},{2,3},{4,5},{5,6},{6,7},{8,9},{9,10},{10,11},{12,13},{... | collective-permute-start | bytes 196616 | tf_op jit(solution)/shard_map/ppermute | solution.py:17
  101.8 6.8 %collective-permute-start.5 = (bf16[1,128,256]{2,1,0:T(8,128)(2,1)S(1)}, bf16[1,128,256]{2,1,0:T(8,128)(2,1)S(1)}, u32[]{:S(2)}, u32[]{:S(2)}) collective-permute-start(bf16[1,128,256]{2,1,0:T(8,128)(2,1)S(1)} %get-tuple-element.18), channel_id=1, source_target_pairs={{4,0},{8,4},{12,8},{16,12},{20,16},{24,20},{28,24},{5,1},{9,5},{13... | collective-permute-start | bytes 196616 | tf_op jit(solution)/shard_map/ppermute | solution.py:19
  106.0 5.6 %collective-permute-start.7 = (bf16[1,128,256]{2,1,0:T(8,128)(2,1)S(1)}, bf16[1,128,256]{2,1,0:T(8,128)(2,1)S(1)}, u32[]{:S(2)}, u32[]{:S(2)}) collective-permute-start(bf16[1,128,256]{2,1,0:T(8,128)(2,1)S(1)} %get-tuple-element.19), channel_id=1, source_target_pairs={{1,0},{2,1},{3,2},{5,4},{6,5},{7,6},{9,8},{10,9},{11,10},{13,12},{... | collective-permute-start | bytes 196616 | tf_op jit(solution)/shard_map/ppermute | solution.py:19
  170.0 1.0 copy-start.1
  176.6 16.8 %collective-permute-start.8 = (bf16[1,128,256]{2,1,0:T(8,128)(2,1)S(1)}, bf16[1,128,256]{2,1,0:T(8,128)(2,1)S(1)}, u32[]{:S(2)}, u32[]{:S(2)}) collective-permute-start(bf16[1,128,256]{2,1,0:T(8,128)(2,1)S(1)} %get-tuple-element.12), channel_id=1, source_target_pairs={{0,4},{4,8},{8,12},{12,16},{16,20},{20,24},{24,28},{1,5},{5,9},{9,... | collective-permute-start | bytes 196616 | tf_op jit(solution)/shard_map/ppermute | solution.py:17
  178.6 14.9 %collective-permute-start.10 = (bf16[1,128,256]{2,1,0:T(8,128)(2,1)S(1)}, bf16[1,128,256]{2,1,0:T(8,128)(2,1)S(1)}, u32[]{:S(2)}, u32[]{:S(2)}) collective-permute-start(bf16[1,128,256]{2,1,0:T(8,128)(2,1)S(1)} %get-tuple-element.13), channel_id=1, source_target_pairs={{0,1},{1,2},{2,3},{4,5},{5,6},{6,7},{8,9},{9,10},{10,11},{12,13},{... | collective-permute-start | bytes 196616 | tf_op jit(solution)/shard_map/ppermute | solution.py:17
  187.0 6.5 %collective-permute-start.9 = (bf16[1,128,256]{2,1,0:T(8,128)(2,1)S(1)}, bf16[1,128,256]{2,1,0:T(8,128)(2,1)S(1)}, u32[]{:S(2)}, u32[]{:S(2)}) collective-permute-start(bf16[1,128,256]{2,1,0:T(8,128)(2,1)S(1)} %get-tuple-element.14), channel_id=1, source_target_pairs={{4,0},{8,4},{12,8},{16,12},{20,16},{24,20},{28,24},{5,1},{9,5},{13... | collective-permute-start | bytes 196616 | tf_op jit(solution)/shard_map/ppermute | solution.py:19
  191.5 5.6 %collective-permute-start.11 = (bf16[1,128,256]{2,1,0:T(8,128)(2,1)S(1)}, bf16[1,128,256]{2,1,0:T(8,128)(2,1)S(1)}, u32[]{:S(2)}, u32[]{:S(2)}) collective-permute-start(bf16[1,128,256]{2,1,0:T(8,128)(2,1)S(1)} %get-tuple-element.15), channel_id=1, source_target_pairs={{1,0},{2,1},{3,2},{5,4},{6,5},{7,6},{9,8},{10,9},{11,10},{13,12},{... | collective-permute-start | bytes 196616 | tf_op jit(solution)/shard_map/ppermute | solution.py:19
  214.5 13.3 %collective-permute-start.12 = (bf16[1,128,256]{2,1,0:T(8,128)(2,1)}, bf16[1,128,256]{2,1,0:T(8,128)(2,1)S(1)}, u32[]{:S(2)}, u32[]{:S(2)}) collective-permute-start(bf16[1,128,256]{2,1,0:T(8,128)(2,1)} %get-tuple-element.8), channel_id=1, source_target_pairs={{0,4},{4,8},{8,12},{12,16},{16,20},{20,24},{24,28},{1,5},{5,9},{9,... | collective-permute-start | bytes 196616 | tf_op jit(solution)/shard_map/ppermute | solution.py:17
  216.4 11.4 %collective-permute-start.14 = (bf16[1,128,256]{2,1,0:T(8,128)(2,1)}, bf16[1,128,256]{2,1,0:T(8,128)(2,1)S(1)}, u32[]{:S(2)}, u32[]{:S(2)}) collective-permute-start(bf16[1,128,256]{2,1,0:T(8,128)(2,1)} %get-tuple-element.9), channel_id=1, source_target_pairs={{0,1},{1,2},{2,3},{4,5},{5,6},{6,7},{8,9},{9,10},{10,11},{12,13},{... | collective-permute-start | bytes 196616 | tf_op jit(solution)/shard_map/ppermute | solution.py:17
  218.3 9.5 %collective-permute-start.13 = (bf16[1,128,256]{2,1,0:T(8,128)(2,1)}, bf16[1,128,256]{2,1,0:T(8,128)(2,1)S(1)}, u32[]{:S(2)}, u32[]{:S(2)}) collective-permute-start(bf16[1,128,256]{2,1,0:T(8,128)(2,1)} %get-tuple-element.10), channel_id=1, source_target_pairs={{4,0},{8,4},{12,8},{16,12},{20,16},{24,20},{28,24},{5,1},{9,5},{13... | collective-permute-start | bytes 196616 | tf_op jit(solution)/shard_map/ppermute | solution.py:19
  222.8 6.2 %collective-permute-start.15 = (bf16[1,128,256]{2,1,0:T(8,128)(2,1)S(1)}, bf16[1,128,256]{2,1,0:T(8,128)(2,1)}, u32[]{:S(2)}, u32[]{:S(2)}) collective-permute-start(bf16[1,128,256]{2,1,0:T(8,128)(2,1)S(1)} %get-tuple-element.11), channel_id=1, source_target_pairs={{1,0},{2,1},{3,2},{5,4},{6,5},{7,6},{9,8},{10,9},{11,10},{13,12},{... | collective-permute-start | bytes 196616 | tf_op jit(solution)/shard_map/ppermute | solution.py:19
  227.8 0.6 copy-start.4
  228.5 0.6 copy-start.5
where the time goes:
time: 244 us; the launch traced here: 243 us
  blocking collectives  90.2 us (37%)
  starting transfers between devices  54.2 us (22%)
  local copies, waits for them, and re-layouts  39.2 us (16%)
  other arithmetic  25.7 us (11%)
  matrix products  23.6 us (10%)
  waiting for transfers between devices  8.78 us (4%)
    psum x2, blocking collectives, per_device(): summed = lax.psum(partial_sum, 'row')  79.6 us
    ppermute x8, starting transfers between devices, padded(): lax.ppermute(tail, axis, [(i, (i + 1) % count) for i in range(ends)])  28.7 us
    ppermute x8, starting transfers between devices, padded(): lax.ppermute(head, axis, [((i + 1) % count, i) for i in range(ends)])  25.5 us
    scatter-add x4, other arithmetic, apply_operator(): jnp.zeros(vector.shape, jnp.float32).at[flat_rows].add(coupling_terms)  18.5 us
    gather x4, local copies, waits for them, and re-layouts, neighbour_faces(): face_vals = vector_b[face_index]  10.6 us
    all_gather x2, blocking collectives, per_device(): lax.all_gather(restricted, 'col', axis=0, tiled=True)  10.6 us
    scatter-add x4, local copies, waits for them, and re-layouts, apply_operator(): jnp.zeros(vector.shape, jnp.float32).at[flat_rows].add(coupling_terms)  10.2 us
    unnamed x19, local copies, waits for them, and re-layouts  9.8 us
  transfers between devices with their start and end apart: 16, of which 3 were waited for; matrix products, arithmetic and copies ran while one was open for 2% of the time, Pallas kernels for 0%

commit v1 on v0

--- a/solution.py
+++ b/solution.py
@@ -58,7 +58,7 @@
             lax.all_gather(restricted, "col", axis=0, tiled=True),
             preferred_element_type=jnp.float32,
         )
-        summed = lax.psum(partial_sum, "row")
+        summed = jnp.sum(lax.all_gather(partial_sum, "row"), axis=0)
         coarse_part = lax.dynamic_slice_in_dim(
             summed, lax.axis_index("row") * block_rows, block_rows, 0
         )

time: 244 us -> 379 us (1.55)
  waiting for transfers between devices: 8.78 us -> 201 us
  blocking collectives: 90.2 us -> 10.8 us
  between operations: 1.01 us -> 14.5 us
  local copies, waits for them, and re-layouts: 39.2 us -> 51.1 us
  starting transfers between devices: 54.2 us -> 48.9 us
    all_gather x0 -> x2, waiting for transfers between devices: none -> 192 us  [per_device(): summed = jnp.sum(lax.all_gather(partial_sum, 'row'), axis=0)]
    psum x2 -> x0, blocking collectives: 79.6 us -> none  [per_device(): summed = lax.psum(partial_sum, 'row')]
    unnamed x19 -> x23, local copies, waits for them, and re-layouts: 9.8 us -> 20.6 us
    ppermute x8, starting transfers between devices: 28.7 us -> 23.7 us  [padded(): lax.ppermute(tail, axis, [(i, (i + 1) % count) for i in range(ends)])]
  transfers between devices with their start and end apart: 16 -> 18, of which waited for: 3 -> 5; matrix products, arithmetic and copies ran while one was open for 2% -> 1% of each run, Pallas kernels for 0% -> 0%
where the time goes in v1:
time: 379 us; the launch traced here: 377 us
  waiting for transfers between devices  201 us (53%)
  local copies, waits for them, and re-layouts  51.1 us (13%)
  starting transfers between devices  48.9 us (13%)
  other arithmetic  29.1 us (8%)
  matrix products  22.4 us (6%)
  between operations  14.5 us (4%)
  blocking collectives  10.8 us (3%)
    all_gather x2, waiting for transfers between devices, per_device(): summed = jnp.sum(lax.all_gather(partial_sum, 'row'), axis=0)  192 us
    ppermute x8, starting transfers between devices, padded(): lax.ppermute(head, axis, [((i + 1) % count, i) for i in range(ends)])  25.1 us
    ppermute x8, starting transfers between devices, padded(): lax.ppermute(tail, axis, [(i, (i + 1) % count) for i in range(ends)])  23.7 us
    unnamed x23, local copies, waits for them, and re-layouts  20.6 us
    scatter-add x4, other arithmetic, apply_operator(): jnp.zeros(vector.shape, jnp.float32).at[flat_rows].add(coupling_terms)  18.5 us
    all_gather x2, blocking collectives, per_device(): lax.all_gather(restricted, 'col', axis=0, tiled=True)  10.8 us
    gather x4, local copies, waits for them, and re-layouts, neighbour_faces(): face_vals = vector_b[face_index]  10.6 us
    scatter-add x4, local copies, waits for them, and re-layouts, apply_operator(): jnp.zeros(vector.shape, jnp.float32).at[flat_rows].add(coupling_terms)  10.2 us
  transfers between devices with their start and end apart: 18, of which 5 were waited for; matrix products, arithmetic and copies ran while one was open for 1% of the time, Pallas kernels for 0%

profile of v1, /device:TPU:9, one launch (start us, length us, event | category | flops | bytes accessed | tf_op | source)
XLA Modules:
  0.0 377.4 jit_solution(10544847201985400444)
XLA Ops:
  8.9 6.1 %all_gather.18 = bf16[384,256]{1,0:T(8,128)(2,1)S(1)} all-gather(bf16[96,256]{1,0:T(8,128)(2,1)S(1)} %convolution_convert_fusion), channel_id=1, replica_groups=mesh['row'=8,'col'=4] {'col'}, dimensions={0}, use_global_device_ids=true | all-gather | bytes 245760 | tf_op jit(solution)/shard_map/all_gather | solution.py:58
  15.0 2.3 convolution_bitcast_fusion.5
  17.5 96.8 %all-gather.5.cloned.1.call-done = f32[6144,256]{0,1:T(8,128)} async-done(((f32[768,256]{0,1:T(8,128)}), f32[6144,256]{0,1:T(8,128)}) %all-gather.5.cloned.1.call-update) | async-done | bytes 6291472 | tf_op jit(solution)/shard_map/all_gather | solution.py:61
  114.3 5.4 %copy.45 = f32[32,8,8,768]{3,2,1,0:T(8,128)S(1)} copy(f32[32,8,8,768]{3,1,2,0:T(8,128)} %bitcast.128) | data formatting | bytes 12582912
  124.9 2.0 gather_fusion
  127.5 2.4 collective-permute-start
  129.9 5.2 %collective-permute-start.2 = (bf16[1,128,256]{2,1,0:T(8,128)(2,1)}, bf16[1,128,256]{2,1,0:T(8,128)(2,1)}, u32[]{:S(2)}, u32[]{:S(2)}) collective-permute-start(bf16[1,128,256]{2,1,0:T(8,128)(2,1)} %get-tuple-element.21), channel_id=1, source_target_pairs={{0,1},{1,2},{2,3},{4,5},{5,6},{6,7},{8,9},{9,10},{10,11},{12,13},{... | collective-permute-start | bytes 196616 | tf_op jit(solution)/shard_map/ppermute | solution.py:17
  135.1 4.0 %collective-permute-start.1 = (bf16[1,128,256]{2,1,0:T(8,128)(2,1)S(1)}, bf16[1,128,256]{2,1,0:T(8,128)(2,1)}, u32[]{:S(2)}, u32[]{:S(2)}) collective-permute-start(bf16[1,128,256]{2,1,0:T(8,128)(2,1)S(1)} %get-tuple-element.22), channel_id=1, source_target_pairs={{4,0},{8,4},{12,8},{16,12},{20,16},{24,20},{28,24},{5,1},{9,5},{13... | collective-permute-start | bytes 196616 | tf_op jit(solution)/shard_map/ppermute | solution.py:19
  139.1 1.9 collective-permute-start.3
  142.6 2.2 collective-permute-done.3
  146.4 4.8 %scatter_custom_fusion = f32[1024,256]{1,0:T(8,128)} fusion(s32[512]{0:T(512)S(1)} %bitcast.139, bf16[512,256]{1,0:T(8,128)(2,1)} %bitcast.131, f32[]{:T(128)} %constant.7.clone.1, f32[512]{0:T(512)S(1)} %bitcast.134), kind=kCustom, calls=%fused_computation.42 | custom fusion | flops 393216 | bytes 1312772 | tf_op jit(solution)/shard_map/scatter-add | solution.py:43
  151.2 2.5 copy.32
  153.8 4.8 %convolution_add_fusion.2 = f32[256,1024]{1,0:T(8,128)} fusion(f32[256,1024]{1,0:T(8,128)} %copy-done.3, bf16[1024,1024]{1,0:T(8,128)(2,1)} %param.9, f32[1024,256]{0,1:T(8,128)S(1)} %copy.33, f32[1024,256]{0,1:T(8,128)} %copy.32, bf16[1024,1024]{1,0:T(8,128)(2,1)S(1)} %copy-done), kind=kOutput, calls=%fused_computation.25 | convolution fusion | flops 1075052544 | bytes 8388608 | tf_op jit(solution)/shard_map/dot_general | solution.py:70
  158.5 2.1 convert_bitcast_fusion.1
  160.6 2.1 copy.34
  162.7 3.3 gather_fusion.1
  166.9 2.2 collective-permute-start.4
  169.2 2.0 collective-permute-start.6
  171.2 4.0 %collective-permute-start.5 = (bf16[1,128,256]{2,1,0:T(8,128)(2,1)S(1)}, bf16[1,128,256]{2,1,0:T(8,128)(2,1)S(1)}, u32[]{:S(2)}, u32[]{:S(2)}) collective-permute-start(bf16[1,128,256]{2,1,0:T(8,128)(2,1)S(1)} %get-tuple-element.18), channel_id=1, source_target_pairs={{4,0},{8,4},{12,8},{16,12},{20,16},{24,20},{28,24},{5,1},{9,5},{13... | collective-permute-start | bytes 196616 | tf_op jit(solution)/shard_map/ppermute | solution.py:19
  175.2 2.6 collective-permute-start.7
  177.8 3.0 collective-permute-done.7
  181.5 4.8 %scatter_custom_fusion.1 = f32[1024,256]{1,0:T(8,128)} fusion(s32[512]{0:T(512)S(1)} %bitcast.140, bf16[512,256]{1,0:T(8,128)(2,1)} %bitcast.132, f32[]{:T(128)} %constant.7.clone.1, f32[512]{0:T(512)S(1)} %bitcast.135), kind=kCustom, calls=%fused_computation.40 | custom fusion | flops 393216 | bytes 1312772 | tf_op jit(solution)/shard_map/scatter-add | solution.py:43
  186.3 2.5 copy.35
  188.9 2.5 fusion.14
  191.4 4.7 %all_gather.21 = bf16[384,256]{1,0:T(8,128)(2,1)S(1)} all-gather(bf16[96,256]{1,0:T(8,128)(2,1)S(1)} %fusion.14), channel_id=1, replica_groups=mesh['row'=8,'col'=4] {'col'}, dimensions={0}, use_global_device_ids=true | all-gather | bytes 245760 | tf_op jit(solution)/shard_map/all_gather | solution.py:58
  196.1 2.4 convolution_bitcast_fusion.4
  198.4 95.1 %all-gather.7.cloned.1.call-done = f32[6144,256]{0,1:T(8,128)} async-done(((f32[768,256]{0,1:T(8,128)}), f32[6144,256]{0,1:T(8,128)}) %all-gather.7.cloned.1.call-update) | async-done | bytes 6291472 | tf_op jit(solution)/shard_map/all_gather | solution.py:61
  293.5 5.4 %copy.46 = f32[32,8,8,768]{3,2,1,0:T(8,128)S(1)} copy(f32[32,8,8,768]{3,1,2,0:T(8,128)} %bitcast.129) | data formatting | bytes 12582912
  302.8 2.1 copy.37
  304.9 2.7 gather_fusion.2
  307.6 2.4 collective-permute-start.8
  310.0 5.2 %collective-permute-start.10 = (bf16[1,128,256]{2,1,0:T(8,128)(2,1)S(1)}, bf16[1,128,256]{2,1,0:T(8,128)(2,1)S(1)}, u32[]{:S(2)}, u32[]{:S(2)}) collective-permute-start(bf16[1,128,256]{2,1,0:T(8,128)(2,1)S(1)} %get-tuple-element.13), channel_id=1, source_target_pairs={{0,1},{1,2},{2,3},{4,5},{5,6},{6,7},{8,9},{9,10},{10,11},{12,13},{... | collective-permute-start | bytes 196616 | tf_op jit(solution)/shard_map/ppermute | solution.py:17
  315.2 4.0 %collective-permute-start.9 = (bf16[1,128,256]{2,1,0:T(8,128)(2,1)S(1)}, bf16[1,128,256]{2,1,0:T(8,128)(2,1)S(1)}, u32[]{:S(2)}, u32[]{:S(2)}) collective-permute-start(bf16[1,128,256]{2,1,0:T(8,128)(2,1)S(1)} %get-tuple-element.14), channel_id=1, source_target_pairs={{4,0},{8,4},{12,8},{16,12},{20,16},{24,20},{28,24},{5,1},{9,5},{13... | collective-permute-start | bytes 196616 | tf_op jit(solution)/shard_map/ppermute | solution.py:19
  321.2 3.6 collective-permute-done.11
  324.8 4.4 %scatter_custom_fusion.2 = f32[1024,256]{1,0:T(8,128)} fusion(s32[512]{0:T(512)S(1)} %bitcast.141, bf16[512,256]{1,0:T(8,128)(2,1)S(1)} %bitcast.133, f32[]{:T(128)} %constant.7.clone.1, f32[512]{0:T(512)S(1)} %bitcast.136), kind=kCustom, calls=%fused_computation.38 | custom fusion | flops 393216 | bytes 1312772 | tf_op jit(solution)/shard_map/scatter-add | solution.py:43
  329.2 2.6 copy.38
  331.8 5.0 %fusion.38 = (bf16[1024,256]{0,1:T(8,128)(2,1)}, f32[1024,256]{0,1:T(8,128)}) fusion(f32[256,1024]{1,0:T(8,128)} %copy-done.1, bf16[1024,1024]{1,0:T(8,128)(2,1)} %param.9, f32[1024,256]{0,1:T(8,128)S(1)} %copy.33, f32[1024,256]{0,1:T(8,128)} %copy.38, bf16[1024,1024]{1,0:T(8,128)(2,1)S(1)} %copy-done), kind=kOutput, calls=%fused_computation.87 | convolution fusion | flops 1075314688 | bytes 8912896 | tf_op jit(solution)/shard_map/dot_general | solution.py:70
  336.8 2.0 copy.40
  338.8 2.7 gather_fusion.3
  342.2 2.2 collective-permute-start.12
  344.4 2.2 collective-permute-start.14
  346.5 4.0 %collective-permute-start.13 = (bf16[1,128,256]{2,1,0:T(8,128)(2,1)}, bf16[1,128,256]{2,1,0:T(8,128)(2,1)S(1)}, u32[]{:S(2)}, u32[]{:S(2)}) collective-permute-start(bf16[1,128,256]{2,1,0:T(8,128)(2,1)} %get-tuple-element.10), channel_id=1, source_target_pairs={{4,0},{8,4},{12,8},{16,12},{20,16},{24,20},{28,24},{5,1},{9,5},{13... | collective-permute-start | bytes 196616 | tf_op jit(solution)/shard_map/ppermute | solution.py:19
  350.5 2.7 collective-permute-start.15
  353.2 2.5 copy.43
  358.0 4.4 %scatter_custom_fusion.3 = f32[1024,256]{1,0:T(8,128)} fusion(s32[512]{0:T(512)S(1)} %bitcast.142, bf16[512,256]{1,0:T(8,128)(2,1)S(1)} %bitcast.130, f32[]{:T(128)} %constant.7.clone.1, f32[512]{0:T(512)S(1)} %bitcast.137), kind=kCustom, calls=%fused_computation.36 | custom fusion | flops 393216 | bytes 1312772 | tf_op jit(solution)/shard_map/scatter-add | solution.py:43
  362.4 2.5 copy.41
  364.9 3.1 fusion.7
  368.1 2.5 copy.44
  (56 shorter events, 21.3 us)
Async XLA Ops:
  7.2 146.6 %copy-start = (bf16[1024,1024]{1,0:T(8,128)(2,1)S(1)}, bf16[1024,1024]{1,0:T(8,128)(2,1)}, u32[]{:S(2)}) copy-start(bf16[1024,1024]{1,0:T(8,128)(2,1)} %param.8) | copy-start | bytes 6291460
  7.2 10.3 %copy-start.8 = (s32[1,4,128]{2,1,0:T(4,128)S(1)}, s32[1,4,128]{2,1,0:T(4,128)}, u32[]{:S(2)}) copy-start(s32[1,4,128]{2,1,0:T(4,128)} %param.13) | copy-start | bytes 6148
  7.2 107.1 %all-gather.5.cloned.1.call-start = ((), (), s32[]{:S(2)}) async-start(), calls=%async_computation | async-start | bytes 7077888 | tf_op jit(solution)/shard_map/all_gather | solution.py:61
  17.4 276.1 %all-gather.7.cloned.1.call-start = ((), (), s32[]{:S(2)}) async-start(), calls=%async_computation.1 | async-start | bytes 7077888 | tf_op jit(solution)/shard_map/all_gather | solution.py:61
  119.7 1.7 copy-start.4
  121.8 1.0 copy-start.3
  126.8 19.6 %copy-start.7 = (f32[1,4,128]{2,1,0:T(4,128)S(1)}, f32[1,4,128]{2,1,0:T(4,128)}, u32[]{:S(2)}) copy-start(f32[1,4,128]{2,1,0:T(4,128)} %param.12) | copy-start | bytes 6148
  127.5 15.1 %collective-permute-start = (bf16[1,128,256]{2,1,0:T(8,128)(2,1)}, bf16[1,128,256]{2,1,0:T(8,128)(2,1)S(1)}, u32[]{:S(2)}, u32[]{:S(2)}) collective-permute-start(bf16[1,128,256]{2,1,0:T(8,128)(2,1)} %get-tuple-element.20), channel_id=1, source_target_pairs={{0,4},{4,8},{8,12},{12,16},{16,20},{20,24},{24,28},{1,5},{5,9},{9,... | collective-permute-start | bytes 196616 | tf_op jit(solution)/shard_map/ppermute | solution.py:17
  129.9 12.7 %collective-permute-start.2 = (bf16[1,128,256]{2,1,0:T(8,128)(2,1)}, bf16[1,128,256]{2,1,0:T(8,128)(2,1)}, u32[]{:S(2)}, u32[]{:S(2)}) collective-permute-start(bf16[1,128,256]{2,1,0:T(8,128)(2,1)} %get-tuple-element.21), channel_id=1, source_target_pairs={{0,1},{1,2},{2,3},{4,5},{5,6},{6,7},{8,9},{9,10},{10,11},{12,13},{... | collective-permute-start | bytes 196616 | tf_op jit(solution)/shard_map/ppermute | solution.py:17
  135.1 7.5 %collective-permute-start.1 = (bf16[1,128,256]{2,1,0:T(8,128)(2,1)S(1)}, bf16[1,128,256]{2,1,0:T(8,128)(2,1)}, u32[]{:S(2)}, u32[]{:S(2)}) collective-permute-start(bf16[1,128,256]{2,1,0:T(8,128)(2,1)S(1)} %get-tuple-element.22), channel_id=1, source_target_pairs={{4,0},{8,4},{12,8},{16,12},{20,16},{24,20},{28,24},{5,1},{9,5},{13... | collective-permute-start | bytes 196616 | tf_op jit(solution)/shard_map/ppermute | solution.py:19
  139.1 5.7 %collective-permute-start.3 = (bf16[1,128,256]{2,1,0:T(8,128)(2,1)S(1)}, bf16[1,128,256]{2,1,0:T(8,128)(2,1)}, u32[]{:S(2)}, u32[]{:S(2)}) collective-permute-start(bf16[1,128,256]{2,1,0:T(8,128)(2,1)S(1)} %get-tuple-element.23), channel_id=1, source_target_pairs={{1,0},{2,1},{3,2},{5,4},{6,5},{7,6},{9,8},{10,9},{11,10},{13,12},{... | collective-permute-start | bytes 196616 | tf_op jit(solution)/shard_map/ppermute | solution.py:19
  166.9 10.8 %collective-permute-start.4 = (bf16[1,128,256]{2,1,0:T(8,128)(2,1)S(1)}, bf16[1,128,256]{2,1,0:T(8,128)(2,1)S(1)}, u32[]{:S(2)}, u32[]{:S(2)}) collective-permute-start(bf16[1,128,256]{2,1,0:T(8,128)(2,1)S(1)} %get-tuple-element.16), channel_id=1, source_target_pairs={{0,4},{4,8},{8,12},{12,16},{16,20},{20,24},{24,28},{1,5},{5,9},{9,... | collective-permute-start | bytes 196616 | tf_op jit(solution)/shard_map/ppermute | solution.py:17
  169.2 8.6 %collective-permute-start.6 = (bf16[1,128,256]{2,1,0:T(8,128)(2,1)S(1)}, bf16[1,128,256]{2,1,0:T(8,128)(2,1)S(1)}, u32[]{:S(2)}, u32[]{:S(2)}) collective-permute-start(bf16[1,128,256]{2,1,0:T(8,128)(2,1)S(1)} %get-tuple-element.17), channel_id=1, source_target_pairs={{0,1},{1,2},{2,3},{4,5},{5,6},{6,7},{8,9},{9,10},{10,11},{12,13},{... | collective-permute-start | bytes 196616 | tf_op jit(solution)/shard_map/ppermute | solution.py:17
  171.2 6.6 %collective-permute-start.5 = (bf16[1,128,256]{2,1,0:T(8,128)(2,1)S(1)}, bf16[1,128,256]{2,1,0:T(8,128)(2,1)S(1)}, u32[]{:S(2)}, u32[]{:S(2)}) collective-permute-start(bf16[1,128,256]{2,1,0:T(8,128)(2,1)S(1)} %get-tuple-element.18), channel_id=1, source_target_pairs={{4,0},{8,4},{12,8},{16,12},{20,16},{24,20},{28,24},{5,1},{9,5},{13... | collective-permute-start | bytes 196616 | tf_op jit(solution)/shard_map/ppermute | solution.py:19
  175.2 5.6 %collective-permute-start.7 = (bf16[1,128,256]{2,1,0:T(8,128)(2,1)S(1)}, bf16[1,128,256]{2,1,0:T(8,128)(2,1)S(1)}, u32[]{:S(2)}, u32[]{:S(2)}) collective-permute-start(bf16[1,128,256]{2,1,0:T(8,128)(2,1)S(1)} %get-tuple-element.19), channel_id=1, source_target_pairs={{1,0},{2,1},{3,2},{5,4},{6,5},{7,6},{9,8},{10,9},{11,10},{13,12},{... | collective-permute-start | bytes 196616 | tf_op jit(solution)/shard_map/ppermute | solution.py:19
  298.9 1.7 copy-start.2
  301.0 1.0 copy-start.1
  307.6 13.5 %collective-permute-start.8 = (bf16[1,128,256]{2,1,0:T(8,128)(2,1)S(1)}, bf16[1,128,256]{2,1,0:T(8,128)(2,1)S(1)}, u32[]{:S(2)}, u32[]{:S(2)}) collective-permute-start(bf16[1,128,256]{2,1,0:T(8,128)(2,1)S(1)} %get-tuple-element.12), channel_id=1, source_target_pairs={{0,4},{4,8},{8,12},{12,16},{16,20},{20,24},{24,28},{1,5},{5,9},{9,... | collective-permute-start | bytes 196616 | tf_op jit(solution)/shard_map/ppermute | solution.py:17
  310.0 11.1 %collective-permute-start.10 = (bf16[1,128,256]{2,1,0:T(8,128)(2,1)S(1)}, bf16[1,128,256]{2,1,0:T(8,128)(2,1)S(1)}, u32[]{:S(2)}, u32[]{:S(2)}) collective-permute-start(bf16[1,128,256]{2,1,0:T(8,128)(2,1)S(1)} %get-tuple-element.13), channel_id=1, source_target_pairs={{0,1},{1,2},{2,3},{4,5},{5,6},{6,7},{8,9},{9,10},{10,11},{12,13},{... | collective-permute-start | bytes 196616 | tf_op jit(solution)/shard_map/ppermute | solution.py:17
  315.2 6.0 %collective-permute-start.9 = (bf16[1,128,256]{2,1,0:T(8,128)(2,1)S(1)}, bf16[1,128,256]{2,1,0:T(8,128)(2,1)S(1)}, u32[]{:S(2)}, u32[]{:S(2)}) collective-permute-start(bf16[1,128,256]{2,1,0:T(8,128)(2,1)S(1)} %get-tuple-element.14), channel_id=1, source_target_pairs={{4,0},{8,4},{12,8},{16,12},{20,16},{24,20},{28,24},{5,1},{9,5},{13... | collective-permute-start | bytes 196616 | tf_op jit(solution)/shard_map/ppermute | solution.py:19
  319.2 5.6 %collective-permute-start.11 = (bf16[1,128,256]{2,1,0:T(8,128)(2,1)S(1)}, bf16[1,128,256]{2,1,0:T(8,128)(2,1)S(1)}, u32[]{:S(2)}, u32[]{:S(2)}) collective-permute-start(bf16[1,128,256]{2,1,0:T(8,128)(2,1)S(1)} %get-tuple-element.15), channel_id=1, source_target_pairs={{1,0},{2,1},{3,2},{5,4},{6,5},{7,6},{9,8},{10,9},{11,10},{13,12},{... | collective-permute-start | bytes 196616 | tf_op jit(solution)/shard_map/ppermute | solution.py:19
  342.2 13.6 %collective-permute-start.12 = (bf16[1,128,256]{2,1,0:T(8,128)(2,1)}, bf16[1,128,256]{2,1,0:T(8,128)(2,1)S(1)}, u32[]{:S(2)}, u32[]{:S(2)}) collective-permute-start(bf16[1,128,256]{2,1,0:T(8,128)(2,1)} %get-tuple-element.8), channel_id=1, source_target_pairs={{0,4},{4,8},{8,12},{12,16},{16,20},{20,24},{24,28},{1,5},{5,9},{9,... | collective-permute-start | bytes 196616 | tf_op jit(solution)/shard_map/ppermute | solution.py:17
  344.4 11.4 %collective-permute-start.14 = (bf16[1,128,256]{2,1,0:T(8,128)(2,1)}, bf16[1,128,256]{2,1,0:T(8,128)(2,1)S(1)}, u32[]{:S(2)}, u32[]{:S(2)}) collective-permute-start(bf16[1,128,256]{2,1,0:T(8,128)(2,1)} %get-tuple-element.9), channel_id=1, source_target_pairs={{0,1},{1,2},{2,3},{4,5},{5,6},{6,7},{8,9},{9,10},{10,11},{12,13},{... | collective-permute-start | bytes 196616 | tf_op jit(solution)/shard_map/ppermute | solution.py:17
  346.5 9.2 %collective-permute-start.13 = (bf16[1,128,256]{2,1,0:T(8,128)(2,1)}, bf16[1,128,256]{2,1,0:T(8,128)(2,1)S(1)}, u32[]{:S(2)}, u32[]{:S(2)}) collective-permute-start(bf16[1,128,256]{2,1,0:T(8,128)(2,1)} %get-tuple-element.10), channel_id=1, source_target_pairs={{4,0},{8,4},{12,8},{16,12},{20,16},{24,20},{28,24},{5,1},{9,5},{13... | collective-permute-start | bytes 196616 | tf_op jit(solution)/shard_map/ppermute | solution.py:19
  350.5 6.5 %collective-permute-start.15 = (bf16[1,128,256]{2,1,0:T(8,128)(2,1)S(1)}, bf16[1,128,256]{2,1,0:T(8,128)(2,1)}, u32[]{:S(2)}, u32[]{:S(2)}) collective-permute-start(bf16[1,128,256]{2,1,0:T(8,128)(2,1)S(1)} %get-tuple-element.11), channel_id=1, source_target_pairs={{1,0},{2,1},{3,2},{5,4},{6,5},{7,6},{9,8},{10,9},{11,10},{13,12},{... | collective-permute-start | bytes 196616 | tf_op jit(solution)/shard_map/ppermute | solution.py:19
  355.8 0.6 copy-start.5
  356.4 0.6 copy-start.6
Sparse Core Ops, SparseCore 0:
  17.5 96.7 all-gather.4
  198.6 94.9 all-gather.6
